TPU v7x, 128 devices: a whole 4x4x4 slice. The times are simulated.
128 devices in a mesh: member: 2 (over x_lo), dp: 64 (over y, x_hi, z, core).
Axes of the slice: x: 4 (x_hi: 2, x_lo: 2; x = x_hi * 2 + x_lo), y: 4, z: 4, core: 2. Of those that a mesh axis runs over, the one named last changes fastest.
Arguments:
- features: bfloat16 [256, 256, 1024], P(('dp', 'member')), may hold values from -10 to 10
- teacher_logits: bfloat16 [4, 256, 256, 256], P('member', 'dp'), may hold values from -320 to 320
- lengths: int32 [256], P(('dp', 'member')), may hold values from 16 to 256
- gain_conv: float32 [1024], replicated, may hold values from 0.5 to 1.5
- weight_in: bfloat16 [1024, 2048], replicated, may hold values from -0.1875 to 0.1875
- weight_depth: float32 [31, 1024], replicated, may hold values from -1 to 1
- weight_out: bfloat16 [1024, 1024], replicated, may hold values from -0.1875 to 0.1875
- gain_out: float32 [1024], replicated, may hold values from 0.5 to 1.5
- head_weight: bfloat16 [1024, 256], replicated, may hold values from -1 to 1
Outputs:
- grad_gain_conv: float32 [1024], replicated
- grad_weight_in: float32 [1024, 2048], replicated
- grad_weight_depth: float32 [31, 1024], replicated
- grad_weight_out: float32 [1024, 1024], replicated
- grad_gain_out: float32 [1024], replicated
- grad_head: float32 [1024, 256], replicated
- utt_loss: float32 [256], P(('dp', 'member'))
All inputs are finite; a program needn't handle non-finite values.
Results may differ from a plain program's by a relative error of at most 0.015.
Values may be sent and summed in bfloat16 or wider, within the bound.
A program may use at most 128 MiB of HBM per device.

v0:
```python
import jax
import jax.numpy as jnp
from jax import lax
from jax.sharding import PartitionSpec as P

TEACHERS = 4


def normalize(values, gain):
    average = jnp.mean(values, axis=-1, keepdims=True)
    centred = values - average
    spread = jnp.mean(centred * centred, axis=-1, keepdims=True)
    return centred * lax.rsqrt(spread + 1e-05) * gain


def live_frames(lengths, frames):
    return (jnp.arange(frames, dtype=jnp.int32)[None, :] < lengths[:, None]).astype(jnp.float32)


def lower_part(conv_weights, features, lengths):
    gain_conv, weight_in, weight_depth, weight_out = conv_weights
    utterances, frames, model_width = features.shape
    widened = features.astype(jnp.float32)
    normed = (
        normalize(widened, gain_conv).astype(jnp.bfloat16).reshape(utterances * frames, model_width)
    )
    projected = jnp.dot(normed, weight_in, preferred_element_type=jnp.float32)
    live_mask = live_frames(lengths, frames)
    gated = (projected[:, :model_width] * jax.nn.sigmoid(projected[:, model_width:])).reshape(
        utterances, frames, model_width
    ) * live_mask[:, :, None]
    half_width = weight_depth.shape[0] // 2
    convolved = lax.conv_general_dilated(
        gated,
        weight_depth[:, None, :],
        (1,),
        [(half_width, half_width)],
        dimension_numbers=("NWC", "WIO", "NWC"),
        feature_group_count=model_width,
        precision=lax.Precision.HIGHEST,
    )
    activated = (
        (convolved * jax.nn.sigmoid(convolved))
        .astype(jnp.bfloat16)
        .reshape(utterances * frames, model_width)
    )
    update = jnp.dot(activated, weight_out, preferred_element_type=jnp.float32)
    return widened + update.reshape(utterances, frames, model_width)


def upper_part(top_weights, residual_sum, target, lengths, mean_frames):
    gain_out, head_weight = top_weights
    utterances, frames, model_width = residual_sum.shape
    final_norm = (
        normalize(residual_sum, gain_out)
        .astype(jnp.bfloat16)
        .reshape(utterances * frames, model_width)
    )
    student_logits = jnp.dot(final_norm, head_weight, preferred_element_type=jnp.float32)
    student_logp = jax.nn.log_softmax(student_logits, axis=-1).reshape(utterances, frames, -1)
    cross_entropy = -jnp.sum(target * student_logp, axis=-1)
    return jnp.sum(cross_entropy * live_frames(lengths, frames), axis=-1) / mean_frames


def student_losses(weights, features, target, lengths, mean_frames):
    residual_sum = lower_part(weights[:4], features, lengths)
    return upper_part(weights[4:], residual_sum, target, lengths, mean_frames)


def teacher_target(summed):
    return jnp.exp(jax.nn.log_softmax(summed / TEACHERS, axis=-1))


def on_device(
    features,
    teacher_logits,
    lengths,
    gain_conv,
    weight_in,
    weight_depth,
    weight_out,
    gain_out,
    head_weight,
):
    frame_total = lax.psum(jnp.sum(lengths.astype(jnp.float32)), ("member", "dp"))
    own_count = lengths.shape[0]
    mean_frames = frame_total / (own_count * lax.axis_size("member") * lax.axis_size("dp"))
    local_sum = jnp.sum(jax.nn.log_softmax(teacher_logits.astype(jnp.float32), axis=-1), axis=0)
    group_sum = lax.psum(local_sum, "member")
    own_sum = lax.dynamic_slice_in_dim(
        group_sum, lax.axis_index("member") * own_count, own_count, 0
    )
    target = teacher_target(own_sum)
    weights = (gain_conv, weight_in, weight_depth, weight_out, gain_out, head_weight)

    def local_loss(trainable):
        return student_losses(trainable, features, target, lengths, mean_frames)

    losses, pullback = jax.vjp(local_loss, weights)
    gradients = pullback(jnp.ones_like(losses))[0]
    totals = lax.psum(
        (
            gradients[0],
            gradients[1].astype(jnp.float32),
            gradients[2],
            gradients[3].astype(jnp.float32),
            gradients[4],
            gradients[5].astype(jnp.float32),
        ),
        ("member", "dp"),
    )
    return (totals[0], totals[1], totals[2], totals[3], totals[4], totals[5], losses)


def solution(mesh):
    in_specs = (
        P(("dp", "member"), None, None),
        P("member", "dp", None, None),
        P(("dp", "member")),
        P(),
        P(),
        P(),
        P(),
        P(),
        P(),
    )
    out_specs = (P(), P(), P(), P(), P(), P(), P(("dp", "member")))
    return jax.shard_map(
        on_device, mesh=mesh, in_specs=in_specs, out_specs=out_specs, check_vma=False
    )
```

profile of v0, /device:TPU:1, one launch (start us, length us, event | category | flops | bytes accessed | tf_op | source)
XLA Modules:
  0.0 415.8 jit_solution(1241103938338909669)
XLA Ops:
  8.9 14.1 %fusion.27 = f32[4,256,256]{2,1,0:T(8,128)} fusion(bf16[2,4,256,256]{3,2,1,0:T(8,128)(2,1)} %param.10, f32[2,4,256]{2,1,0:T(4,128)S(1)} %reduce_max.36), kind=kOutput, calls=%fused_computation.43 | output fusion | flops 2885887 | bytes 2105344 | tf_op jit(solution)/shard_map/jit(log_softmax)/reduce_sum | solution.py:88
  23.7 69.0 %psum.57 = f32[]{:T(128)} all-reduce(f32[]{:T(128)} %convert_reduce_fusion.1), channel_id=1, replica_groups=mesh['member'=2,'dp'=64] {'member','dp'}, use_global_device_ids=true, to_apply=%region_9.10 | all-reduce | flops 1 | bytes 8 | tf_op jit(solution)/shard_map/psum | solution.py:85
  95.2 2.4 fusion.73
  101.2 1.6 copy.69
  104.2 1.9 fusion.3
  106.1 11.0 %multiply_convert_fusion = (bf16[16,36,1024]{2,0,1:T(8,128)(2,1)S(1)}, f32[16,36,1024]{2,0,1:T(8,128)}, f32[16,36,1024]{2,0,1:T(8,128)}, f32[16,36,1024]{2,0,1:T(8,128)}) fusion(f32[31,1,1024]{2,0,1:T(8,128)S(1)} %bitcast.83, f32[2,8,66,1024]{3,0,2,1:T(2,128)S(1)} %fusion.3, pred[16,36]{0,1:T(8,128)(4,1)S(1)} %copy-done.32), kind=kOutput, calls=%fused_computation.32 | convolution fusion | flops 224133120 | bytes 12710464 | tf_op jit(solution)/shard_map/jvp()/conv_general_dilated | solution.py:33
  117.2 1.7 copy.49
  118.9 2.7 reshape.152
  121.6 2.6 fusion.71
  128.1 2.9 copy.56
  130.9 2.9 reshape.165
  133.8 1.7 copy-done.20
  135.5 2.9 copy.50
  138.3 2.9 reshape.161
  141.2 1.7 copy-done.19
  142.9 2.9 copy.53
  145.7 3.0 reshape.163
  149.5 2.0 subtract_subtract_fusion
  152.8 2.1 fusion.70
  162.7 9.6 %fusion.31 = f32[2,256,1024]{2,0,1:T(2,128)S(1)} fusion(f32[2,256,1024]{2,1,0:T(8,128)S(1)} %slice-done, f32[2,256,1024]{2,1,0:T(8,128)S(1)} %slice-done.2, f32[2,256,1024]{2,1,0:T(8,128)S(1)} %slice-done.1, f32[2,256,1024]{2,1,0:T(8,128)S(1)} %convert.9), kind=kLoop, calls=%fused_computation.50 | loop fusion | flops 2097152 | bytes 10485760 | tf_op jit(solution)/shard_map/transpose(jvp())/add_any | solution.py:43
  172.2 27.8 %fusion.68 = f32[31,1,1024]{2,1,0:T(1,128)S(1)} fusion(f32[2,256,1024]{2,0,1:T(2,128)S(1)} %fusion.31, f32[2,256,1024]{2,1,0:T(8,128)S(1)} %copy-done.12), kind=kOutput, calls=%fused_computation.115 | convolution fusion | flops 189136896 | bytes 4321280 | tf_op jit(solution)/shard_map/transpose(jvp())/conv_general_dilated | solution.py:33
  201.3 3.3 fusion.35
  206.9 5.5 %fusion.39 = f32[16,36,1024]{2,0,1:T(8,128)S(1)} fusion(f32[2,7,30,1024]{3,1,0,2:T(8,128)S(1)} %slice.22, f32[2,8,36,1024]{3,1,0,2:T(8,128)S(1)} %copy.59, pred[16,36]{0,1:T(8,128)(4,1)S(1)} %copy-done.32, f32[31,1024,1]{1,0,2:T(8,128)S(1)} %bitcast.84), kind=kOutput, calls=%fused_computation.67 | convolution fusion | flops 223248384 | bytes 6566464 | tf_op jit(solution)/shard_map/transpose(jvp())/conv_general_dilated | solution.py:33
  212.3 2.9 copy.61
  215.2 3.1 reshape.159
  218.3 1.9 slice_multiply_fusion
  222.3 5.8 %convert_convert_fusion = f32[1024,2048]{1,0:T(8,128)} fusion(bf16[512,1024]{1,0:T(8,128)(2,1)S(1)} %bitcast.80, f32[512,1024]{1,0:T(8,128)S(1)} %get-tuple-element.18, f32[512,1024]{1,0:T(8,128)S(1)} %get-tuple-element.17), kind=kOutput, calls=%fused_computation.15 | convolution fusion | flops 2152726528 | bytes 13631488 | tf_op jit(solution)/shard_map/transpose(jvp())/dot_general | solution.py:27
  229.7 5.2 %fusion.22 = f32[1024]{0:T(1024)S(1)} fusion(bf16[2,256,1024]{2,1,0:T(8,128)(2,1)S(1)} %copy-done.6, f32[2,256]{1,0:T(2,128)S(1)} %add_rsqrt_fusion, f32[2,256]{1,0:T(2,128)S(1)} %broadcast_multiply_fusion.3, bf16[1024,2048]{1,0:T(8,128)(2,1)} %param.13, f32[512,1024]{1,0:T(8,128)} %copy-done.15, f32[512,1024]{1,0:T(8,128)S(1)} %copy-done.14), kind=kOutput, calls=%fused_computation.37 | convolution fusion | flops 2152201216 | bytes 9445376 | tf_op jit(solution)/shard_map/transpose(jvp())/dot_general | solution.py:27
  234.9 63.3 %all-reduce.2 = (f32[1024]{0:T(1024)}, f32[1024]{0:T(1024)}) all-reduce(f32[1024]{0:T(1024)S(1)} %fusion.22, f32[1024]{0:T(1024)S(1)} %get-tuple-element.7), channel_id=1, replica_groups=mesh['member'=2,'dp'=64] {'member','dp'}, use_global_device_ids=true, to_apply=%region_18.19 | all-reduce | flops 2048 | bytes 16384 | tf_op jit(solution)/shard_map/psum | solution.py:101
  299.0 97.3 %all-reduce.9.cloned.1.call-done = (f32[1024,2048]{1,0:T(8,128)}, f32[31,1024]{1,0:T(8,128)}, f32[1024,1024]{1,0:T(8,128)}, f32[1024,256]{1,0:T(8,128)}) async-done(((f32[1024,2048]{1,0:T(8,128)}, f32[31,1024]{1,0:T(8,128)}, f32[1024,1024]{1,0:T(8,128)}, f32[1024,256]{1,0:T(8,128)}), (f32[1024,2048]{1,0:T(8,128)}, f32[31,1024]{1,0:T(8,128)}, f32[1024,1024]{1,0:T(8,128)}, ...) | async-done | bytes 13758480 | tf_op jit(solution)/shard_map/psum | solution.py:101
  396.3 8.0 %copy.104 = f32[1024,2048]{1,0:T(8,128)} copy(f32[1024,2048]{1,0:T(8,128)} %get-tuple-element.29) | data formatting | bytes 16777216
  405.0 2.1 copy.106
  (119 shorter events, 32.9 us)
Async XLA Ops:
  7.2 114.4 %copy-start = (bf16[1024,1024]{1,0:T(8,128)(2,1)S(1)}, bf16[1024,1024]{1,0:T(8,128)(2,1)}, u32[]{:S(2)}) copy-start(bf16[1024,1024]{1,0:T(8,128)(2,1)} %param.15) | copy-start | bytes 6291460
  7.2 144.3 %all-reduce.7.cloned.1.call-start = ((), (), s32[]{:S(2)}) async-start(), calls=%async_computation | async-start | bytes 2097152 | tf_op jit(solution)/shard_map/psum | solution.py:89
  8.8 14.2 %copy-start.29 = (s32[2]{0:T(128)S(1)}, s32[2]{0:T(128)}, u32[]{:S(2)}) copy-start(s32[2]{0:T(128)} %param.11) | copy-start | bytes 28
  8.9 83.8 %copy-start.6 = (bf16[2,256,1024]{2,1,0:T(8,128)(2,1)S(1)}, bf16[2,256,1024]{2,1,0:T(8,128)(2,1)}, u32[]{:S(2)}) copy-start(bf16[2,256,1024]{2,1,0:T(8,128)(2,1)} %param.9) | copy-start | bytes 3145732
  22.9 70.4 %copy-start.30 = (f32[1024]{0:T(1024)S(1)}, f32[1024]{0:T(1024)}, u32[]{:S(2)}) copy-start(f32[1024]{0:T(1024)} %param.12) | copy-start | bytes 12292
  23.0 373.3 %all-reduce.9.cloned.1.call-start = ((), (), s32[]{:S(2)}) async-start(), calls=%async_computation.1 | async-start | bytes 27525120 | tf_op jit(solution)/shard_map/psum | solution.py:101
  92.7 2.6 copy-start.18
  97.6 2.0 copy-start.4
  99.8 1.4 copy-start.11
  104.2 1.9 copy-start.31
  104.2 1.9 copy-start.32
  124.2 1.3 copy-start.2
  124.6 1.9 copy-start.22
  125.5 2.5 copy-start.21
  133.8 1.7 copy-start.20
  141.2 1.7 copy-start.19
  151.5 3.5 copy-start.10
  151.5 3.7 copy-start.8
  155.0 1.7 copy-start.23
  155.3 2.0 copy-start.3
  159.5 1.6 slice-start.1
  159.5 2.2 slice-start.2
  160.8 1.8 slice-start
  162.7 9.6 %copy-start.12 = (f32[2,256,1024]{2,1,0:T(8,128)S(1)}, f32[2,256,1024]{2,1,0:T(8,128)}, u32[]{:S(2)}) copy-start(f32[2,256,1024]{2,1,0:T(8,128)} %copy-done.11) | copy-start | bytes 6291460
  218.3 2.8 copy-start.5
  222.1 6.0 %copy-start.13 = (f32[512,1024]{1,0:T(8,128)}, f32[512,1024]{1,0:T(8,128)S(1)}, u32[]{:S(2)}) copy-start(f32[512,1024]{1,0:T(8,128)S(1)} %get-tuple-element.17) | copy-start | bytes 6291460
  222.1 6.0 %copy-start.15 = (f32[512,1024]{1,0:T(8,128)}, f32[512,1024]{1,0:T(8,128)S(1)}, u32[]{:S(2)}) copy-start(f32[512,1024]{1,0:T(8,128)S(1)} %get-tuple-element.18) | copy-start | bytes 6291460
  228.1 1.6 copy-start.14
  396.3 8.0 %copy-start.27 = (f32[31,1024]{1,0:T(8,128)S(1)}, f32[31,1024]{1,0:T(8,128)}, u32[]{:S(2)}) copy-start(f32[31,1024]{1,0:T(8,128)} %get-tuple-element.30) | copy-start | bytes 380932
  396.3 8.7 %copy-start.17 = (f32[1024,1024]{1,0:T(8,128)S(1)}, f32[1024,1024]{1,0:T(8,128)}, u32[]{:S(2)}) copy-start(f32[1024,1024]{1,0:T(8,128)} %get-tuple-element.31) | copy-start | bytes 12582916
  405.0 2.1 copy-start.26
  405.0 3.8 copy-start.1
  (6 other events, 6.0 us)
Sparse Core Ops, SparseCore 0:
  23.1 50.1 all-reduce.6
  228.3 167.9 all-reduce.8
where the time goes:
time: 419 us; the launch traced here: 416 us
  blocking collectives  132 us (32%)
  waiting for transfers between devices  97.3 us (23%)
  matrix products  67.2 us (16%)
  local copies, waits for them, and re-layouts  60.9 us (15%)
  other arithmetic  42.6 us (10%)
  between operations  15.5 us (4%)
    psum x1, waiting for transfers between devices, on_device(): lax.psum((gradients[0], gradients[1].astype(jnp.float32), gradients[2], g...  97.3 us
    psum x1, blocking collectives, on_device(): lax.psum(jnp.sum(lengths.astype(jnp.float32)), ('member', 'dp'))  69 us
    psum x1, blocking collectives, on_device(): lax.psum((gradients[0], gradients[1].astype(jnp.float32), gradients[2], g...  63.3 us
    conv_general_dilated x3, matrix products, lower_part(): lax.conv_general_dilated(gated, weight_depth[:, None, :], (1,), [(half_wi...  44.3 us
    unnamed x73, local copies, waits for them, and re-layouts  27.9 us
    conv_general_dilated x9, local copies, waits for them, and re-layouts, lower_part(): lax.conv_general_dilated(gated, weight_depth[:, None, :], (1,), [(half_wi...  14.6 us
    reduce_sum x1, other arithmetic, on_device(): jax.nn.log_softmax(teacher_logits.astype(jnp.float32), axis=-1)  14.1 us
    dot_general x3, matrix products, lower_part(): projected = jnp.dot(normed, weight_in, preferred_element_type=jnp.float32)  13.4 us
  transfers between devices with their start and end apart: 2, of which 1 were waited for; matrix products, arithmetic and copies ran while one was open for 13% of the time, Pallas kernels for 0%

commit v1 on v0

--- a/solution.py
+++ b/solution.py
@@ -4,6 +4,11 @@
 from jax.sharding import PartitionSpec as P
 
 TEACHERS = 4
+
+
+def by_each_axis(x, first, second):
+    partial = lax.psum(x, first)
+    return lax.psum(partial, second)
 
 
 def normalize(values, gain):
@@ -98,7 +103,7 @@
 
     losses, pullback = jax.vjp(local_loss, weights)
     gradients = pullback(jnp.ones_like(losses))[0]
-    totals = lax.psum(
+    totals = by_each_axis(
         (
             gradients[0],
             gradients[1].astype(jnp.float32),
@@ -107,7 +112,8 @@
             gradients[4],
             gradients[5].astype(jnp.float32),
         ),
-        ("member", "dp"),
+        "dp",
+        "member",
     )
     return (totals[0], totals[1], totals[2], totals[3], totals[4], totals[5], losses)
 

time: 419 us -> 1250 us (2.98)
  waiting for transfers between devices: 97.3 us -> 818 us
  blocking collectives: 132 us -> 244 us
    psum x1 -> x2, waiting for transfers between devices: 97.3 us -> 818 us  [the longest x1 674 us: by_each_axis(): partial = lax.psum(x, first)]
    psum x1 -> x2, blocking collectives: 63.3 us -> 175 us  [the longest x1 170 us: by_each_axis(): partial = lax.psum(x, first)]
  transfers between devices with their start and end apart: 2 -> 3, of which waited for: 1 -> 2; matrix products, arithmetic and copies ran while one was open for 13% -> 4% of each run, Pallas kernels for 0% -> 0%
where the time goes in v1:
time: 1250 us
  waiting for transfers between devices  818 us (65%)
  blocking collectives  244 us (20%)
  matrix products  67.2 us (5%)
  local copies, waits for them, and re-layouts  60.9 us (5%)
  other arithmetic  42.6 us (3%)
  between operations  15.2 us (1%)
    psum x1, waiting for transfers between devices, by_each_axis(): partial = lax.psum(x, first)  674 us
    psum x1, blocking collectives, by_each_axis(): partial = lax.psum(x, first)  170 us
    psum x1, waiting for transfers between devices, by_each_axis(): return lax.psum(partial, second)  144 us
    psum x1, blocking collectives, on_device(): lax.psum(jnp.sum(lengths.astype(jnp.float32)), ('member', 'dp'))  69 us
    conv_general_dilated x3, matrix products, lower_part(): lax.conv_general_dilated(gated, weight_depth[:, None, :], (1,), [(half_wi...  44.3 us
    unnamed x73, local copies, waits for them, and re-layouts  27.9 us
  transfers between devices with their start and end apart: 3, of which 2 were waited for; matrix products, arithmetic and copies ran while one was open for 4% of the time, Pallas kernels for 0%

profile of v1, /device:TPU:1, one launch (start us, length us, event | category | flops | bytes accessed | tf_op | source)
XLA Modules:
  0.0 1248.3 jit_solution(15701344253762218985)
XLA Ops:
  8.9 14.1 %fusion.27 = f32[4,256,256]{2,1,0:T(8,128)} fusion(bf16[2,4,256,256]{3,2,1,0:T(8,128)(2,1)} %param.10, f32[2,4,256]{2,1,0:T(4,128)S(1)} %reduce_max.36), kind=kOutput, calls=%fused_computation.43 | output fusion | flops 2885887 | bytes 2105344 | tf_op jit(solution)/shard_map/jit(log_softmax)/reduce_sum | solution.py:93
  23.7 69.0 %psum.99 = f32[]{:T(128)} all-reduce(f32[]{:T(128)} %convert_reduce_fusion.1), channel_id=1, replica_groups=mesh['member'=2,'dp'=64] {'member','dp'}, use_global_device_ids=true, to_apply=%region_9.10 | all-reduce | flops 1 | bytes 8 | tf_op jit(solution)/shard_map/psum | solution.py:90
  95.2 2.4 fusion.73
  104.3 1.9 fusion.3
  106.1 11.0 multiply_convert_fusion
  117.2 1.7 copy.49
  118.9 2.7 reshape.152
  121.6 2.6 fusion.71
  128.1 2.9 copy.56
  130.9 2.9 reshape.165
  133.8 1.7 copy-done.20
  135.5 2.9 copy.50
  138.3 2.9 reshape.161
  142.9 2.9 copy.53
  145.8 3.0 reshape.163
  149.5 2.0 subtract_subtract_fusion
  152.8 2.1 fusion.70
  162.7 9.6 fusion.31
  172.2 27.8 %fusion.68 = f32[31,1,1024]{2,1,0:T(1,128)S(1)} fusion(f32[2,256,1024]{2,0,1:T(2,128)S(1)} %fusion.31, f32[2,256,1024]{2,1,0:T(8,128)S(1)} %copy-done.12), kind=kOutput, calls=%fused_computation.115 | convolution fusion | flops 189136896 | bytes 4321280 | tf_op jit(solution)/shard_map/transpose(jvp())/conv_general_dilated | solution.py:38
  201.3 3.3 fusion.35
  206.9 5.5 fusion.39
  212.4 2.9 copy.61
  215.2 3.1 reshape.159
  218.3 1.9 slice_multiply_fusion
  222.3 5.8 convert_convert_fusion
  228.2 674.1 %all-reduce.12.cloned.1.call-done = (f32[1024,2048]{1,0:T(8,128)}, f32[31,1024]{1,0:T(8,128)}, f32[1024,1024]{1,0:T(8,128)}, f32[1024,256]{1,0:T(8,128)}) async-done(((f32[1024,2048]{1,0:T(8,128)}, f32[31,1024]{1,0:T(8,128)}, f32[1024,1024]{1,0:T(8,128)}, f32[1024,256]{1,0:T(8,128)}), (f32[1024,2048]{1,0:T(8,128)}, f32[31,1024]{1,0:T(8,128)}, f32[1024,1024]{1,0:T(8,128)}, ...) | async-done | bytes 13758480 | tf_op jit(solution)/shard_map/psum | solution.py:10
  903.9 5.2 fusion.22
  909.1 170.3 %all-reduce.2 = (f32[1024]{0:T(1024)S(1)}, f32[1024]{0:T(1024)S(1)}) all-reduce(f32[1024]{0:T(1024)S(1)} %fusion.22, f32[1024]{0:T(1024)S(1)} %get-tuple-element.7), channel_id=1, replica_groups=mesh['member'=2,'dp'=64] {'dp'}, use_global_device_ids=true, to_apply=%region_18.19 | all-reduce | flops 2048 | bytes 16384 | tf_op jit(solution)/shard_map/psum | solution.py:10
  1079.4 5.0 all-reduce.4
  1085.1 143.9 %all-reduce.14.cloned.1.call-done = (f32[1024,2048]{1,0:T(8,128)}, f32[31,1024]{1,0:T(8,128)}, f32[1024,1024]{1,0:T(8,128)}, f32[1024,256]{1,0:T(8,128)}) async-done(((f32[1024,2048]{1,0:T(8,128)}, f32[31,1024]{1,0:T(8,128)}, f32[1024,1024]{1,0:T(8,128)}, f32[1024,256]{1,0:T(8,128)}), (f32[1024,2048]{1,0:T(8,128)}, f32[31,1024]{1,0:T(8,128)}, f32[1024,1024]{1,0:T(8,128)}, ...) | async-done | bytes 13758480 | tf_op jit(solution)/shard_map/psum | solution.py:11
  1229.0 8.0 copy.108
  1237.7 2.1 copy.110
  (123 shorter events, 36.2 us)
Async XLA Ops:
  7.2 114.4 %copy-start = (bf16[1024,1024]{1,0:T(8,128)(2,1)S(1)}, bf16[1024,1024]{1,0:T(8,128)(2,1)}, u32[]{:S(2)}) copy-start(bf16[1024,1024]{1,0:T(8,128)(2,1)} %param.15) | copy-start | bytes 6291460
  7.2 144.4 %all-reduce.10.cloned.1.call-start = ((), (), s32[]{:S(2)}) async-start(), calls=%async_computation | async-start | bytes 2097152 | tf_op jit(solution)/shard_map/psum | solution.py:94
  8.8 14.2 %copy-start.29 = (s32[2]{0:T(128)S(1)}, s32[2]{0:T(128)}, u32[]{:S(2)}) copy-start(s32[2]{0:T(128)} %param.11) | copy-start | bytes 28
  8.9 83.8 %copy-start.6 = (bf16[2,256,1024]{2,1,0:T(8,128)(2,1)S(1)}, bf16[2,256,1024]{2,1,0:T(8,128)(2,1)}, u32[]{:S(2)}) copy-start(bf16[2,256,1024]{2,1,0:T(8,128)(2,1)} %param.9) | copy-start | bytes 3145732
  22.9 70.4 %copy-start.30 = (f32[1024]{0:T(1024)S(1)}, f32[1024]{0:T(1024)}, u32[]{:S(2)}) copy-start(f32[1024]{0:T(1024)} %param.12) | copy-start | bytes 12292
  23.0 879.3 %all-reduce.12.cloned.1.call-start = ((), (), s32[]{:S(2)}) async-start(), calls=%async_computation.1 | async-start | bytes 27525120 | tf_op jit(solution)/shard_map/psum | solution.py:10
  92.7 2.6 copy-start.18
  97.6 2.0 copy-start.4
  99.8 1.4 copy-start.11
  104.2 1.9 copy-start.31
  104.2 1.9 copy-start.32
  124.6 1.9 copy-start.22
  125.5 2.5 copy-start.21
  133.8 1.7 copy-start.20
  141.2 1.7 copy-start.19
  151.5 3.5 copy-start.10
  151.5 3.7 copy-start.8
  155.0 1.7 copy-start.23
  155.3 2.0 copy-start.3
  159.5 1.6 slice-start.1
  159.5 2.2 slice-start.2
  160.8 1.8 slice-start
  162.7 9.6 copy-start.12
  218.3 2.8 copy-start.5
  222.1 6.0 copy-start.13
  222.1 6.0 copy-start.15
  228.2 1000.8 %all-reduce.14.cloned.1.call-start = ((), (), s32[]{:S(2)}) async-start(), calls=%async_computation.2 | async-start | bytes 27525120 | tf_op jit(solution)/shard_map/psum | solution.py:11
  902.3 1.6 copy-start.14
  1229.0 8.0 copy-start.27
  1229.0 8.7 copy-start.17
  1237.7 2.1 copy-start.26
  1237.7 3.8 copy-start.1
  (7 other events, 7.3 us)
Sparse Core Ops, SparseCore 0:
  23.1 50.1 all-reduce.9
  228.3 673.9 all-reduce.11
  905.5 323.4 all-reduce.13
